TPU v7x, 32 devices: a whole 2x2x4 slice. The times are simulated.
32 devices in a mesh: virt: 8 (over y, x, core), occ: 4 (over z).
Axes of the slice: x: 2, y: 2, z: 4, core: 2. Of those that a mesh axis runs over, the one named last changes fastest.
Arguments:
- amplitudes: bfloat16 [512, 4096], P('occ', 'virt'), may hold values from -6 to 6
- integrals: bfloat16 [1024, 16384], P(None, 'virt'), may hold values from -0.1875 to 0.1875
- panel_owner: int32 [4, 2], P('occ'), may hold values from 0 to 7, as said below
- inter: bfloat16 [8192, 8192], P('occ', 'virt'), may hold values from -0.125 to 0.125
- dest: int32 [4, 8, 16], P('occ', 'virt'), may hold values from 0 to 3, as said below
- screen: int32 [4, 8, 16], P('occ', 'virt'), may hold values from 0 to 1
Outputs:
- contracted: bfloat16 [512, 8192], P('occ', 'virt')
Inputs may be any that keep to these rules, and one draw needn't show every extreme that they name: `panel_owner`: in each row the 2 entries are distinct. `dest`: among the subtiles of one device that screen marks 1, no two name the same owner.
All inputs are finite; a program needn't handle non-finite values.
Results may differ from a plain program's by a relative error of at most 0.0055.
Values may be sent and summed in bfloat16 or wider, within the bound.
A program may use at most 64 MiB of HBM per device.

v0:
```python
import jax
import jax.numpy as jnp
from jax import lax
from jax.sharding import PartitionSpec as P

SROWS = 32


def on_device(amplitudes, integrals, panel_owner, inter, dest, screen):
    op_rows = amplitudes.shape[0]
    tile = amplitudes.shape[1]
    cols = integrals.shape[1]
    steps = panel_owner.shape[1]
    n_sub = dest.shape[2]
    n_occ = lax.axis_size("occ")
    half_splits = op_rows // SROWS
    col_tiles = cols // tile
    every = lax.all_gather(amplitudes[None], "virt", axis=0, tiled=True)
    chosen_entries = jnp.take(every, panel_owner[0], axis=0)
    chosen_entries = chosen_entries.transpose(1, 0, 2).reshape(op_rows, steps * tile)
    accum = jnp.dot(chosen_entries, integrals, preferred_element_type=jnp.float32)
    ladder = accum.astype(jnp.bfloat16)
    subtiles = (
        ladder.reshape(half_splits, SROWS, col_tiles, tile)
        .transpose(0, 2, 1, 3)
        .reshape(n_sub, SROWS, tile)
    )
    owners = jnp.arange(n_occ, dtype=jnp.int32)
    labels = jnp.arange(1, n_sub + 1, dtype=jnp.int32)
    routing = (dest[0, 0][None, :] == owners[:, None]) & (screen[0, 0][None, :] == 1)
    outgoing = jnp.einsum(
        "os,srt->ort", routing.astype(jnp.bfloat16), subtiles, preferred_element_type=jnp.float32
    ).astype(jnp.bfloat16)
    output_marker = jnp.sum(routing.astype(jnp.int32) * labels[None, :], axis=1).astype(
        jnp.bfloat16
    )[:, None]
    arriving_tiles, tag_in = (
        lax.all_to_all(outgoing, "occ", split_axis=0, concat_axis=0, tiled=True),
        lax.all_to_all(output_marker, "occ", split_axis=0, concat_axis=0, tiled=True),
    )
    choose_surviving = tag_in.astype(jnp.float32) == labels[None, :].astype(jnp.float32)
    summed = jnp.einsum(
        "ez,ead->zad",
        choose_surviving.astype(jnp.bfloat16),
        arriving_tiles,
        preferred_element_type=jnp.float32,
    )
    gathered = summed.astype(jnp.bfloat16)
    left = (
        gathered.reshape(half_splits, col_tiles, SROWS, tile)
        .transpose(0, 2, 1, 3)
        .reshape(op_rows, cols)
    )
    return jnp.dot(left, inter, preferred_element_type=jnp.float32).astype(jnp.bfloat16)


def solution(mesh):
    return jax.shard_map(
        on_device,
        mesh=mesh,
        in_specs=(
            P("occ", "virt"),
            P(None, "virt"),
            P("occ", None),
            P("occ", "virt"),
            P("occ", "virt", None),
            P("occ", "virt", None),
        ),
        out_specs=P("occ", "virt"),
        check_vma=False,
    )
```

profile of v0, /device:TPU:0, one launch (start us, length us, event | category | flops | bytes accessed | tf_op | source)
XLA Modules:
  0.0 64.2 jit_solution(17440745688563391463)
XLA Ops:
  6.5 0.0 all-gather.3.cloned.1.call-start
  6.5 0.7 %all-gather.3.cloned.1.call-update = ((bf16[128,512]{1,0:T(8,128)(2,1)}), bf16[1024,512]{1,0:T(8,128)(2,1)}) async-update(((), (), s32[]{:S(2)}) %all-gather.3.cloned.1.call-start, bf16[128,512]{1,0:T(8,128)(2,1)} %param.6) | async-update | bytes 1310744
  7.3 0.7 %compare_bitcast_fusion = pred[16]{0:T(512)(128)(4,1)S(1)} fusion(s32[1,1,16]{2,1,0:T(1,128)} %param.11), kind=kLoop, calls=%fused_computation.19 | loop fusion | flops 16 | bytes 80 | tf_op jit(solution)/shard_map/eq | solution.py:30
  7.9 0.8 %select_reduce_fusion = s32[4]{0:T(128)S(1)} fusion(s32[16]{0:T(128)S(1)} %iota_add_fusion, s32[16]{0:T(128)} %bitcast.39, pred[16]{0:T(512)(128)(4,1)S(1)} %compare_bitcast_fusion), kind=kLoop, calls=%fused_computation.12 | loop fusion | flops 252 | bytes 160 | tf_op jit(solution)/shard_map/reduce_sum | solution.py:34
  8.7 0.7 %copy.20 = bf16[4,1,1]{2,1,0:T(2,128)(2,1)} copy(bf16[4,1,1]{0,2,1:T(2,128)(2,1)S(1)} %convert_bitcast_fusion) | data formatting | bytes 16 | tf_op jit(solution)/shard_map/convert_element_type | solution.py:34
  9.4 6.3 %all-to-all-start = ((bf16[4,1,1]{2,1,0:T(2,128)(2,1)}), bf16[4,1,1]{2,1,0:T(2,128)(2,1)S(1)}, u32[]{:S(2)}, u32[]{:S(2)}) async-start(bf16[4,1,1]{2,1,0:T(2,128)(2,1)} %copy.20), calls=%async_computation | async-start | bytes 4096 | tf_op jit(solution)/shard_map/all_to_all | solution.py:39
  15.7 0.7 %fusion.11 = s32[2]{0:T(128)S(1)} fusion(s32[1,2]{1,0:T(1,128)} %param.8), kind=kLoop, calls=%fused_computation.24 | loop fusion | flops 6 | bytes 16 | tf_op jit(solution)/shard_map/jit(_take)/jit(_where)/select_n | solution.py:19
  16.4 0.7 %compare_and_fusion = pred[2]{0:T(512)(128)(4,1)S(1)} fusion(s32[1,2]{1,0:T(1,128)} %param.8), kind=kLoop, calls=%fused_computation.17 | loop fusion | flops 12 | bytes 10 | tf_op jit(solution)/shard_map/jit(_take)/and | solution.py:19
  17.1 18.3 %all-gather.3.cloned.1.call-done = bf16[1024,512]{1,0:T(8,128)(2,1)} async-done(((bf16[128,512]{1,0:T(8,128)(2,1)}), bf16[1024,512]{1,0:T(8,128)(2,1)}) %all-gather.3.cloned.1.call-update) | async-done | bytes 1048592 | tf_op jit(solution)/shard_map/all_gather | solution.py:18
  35.3 1.8 %gather_fusion = bf16[2,128,512]{2,1,0:T(8,128)(2,1)S(1)} fusion(bf16[8,128,512]{2,1,0:T(8,128)(2,1)} %bitcast.38, s32[1024]{0:T(1024)S(1)} %pad_clamp_fusion), kind=kCustom, calls=%fused_computation | custom fusion | bytes 524296 | tf_op jit(solution)/shard_map/jit(_take)/gather | solution.py:19
  37.1 0.0 copy-start
  37.2 0.1 select_bitcast_fusion
  37.2 0.2 copy.21
  37.4 2.9 %convolution_convert_fusion = bf16[128,2048]{1,0:T(8,128)(2,1)S(1)} fusion(bf16[128,1024]{0,1:T(8,128)(2,1)S(1)} %bitcast.37, bf16[1024,2048]{1,0:T(8,128)(2,1)} %param.7), kind=kOutput, calls=%fused_computation.1 | convolution fusion | flops 537133056 | bytes 4980736 | tf_op jit(solution)/shard_map/dot_general | solution.py:21
  40.4 0.4 reshape.88
  40.7 0.1 copy.22
  40.9 0.0 copy-done
  40.9 0.4 convolution_convert_fusion.3
  41.3 0.7 %copy.24 = bf16[4,32,512]{2,1,0:T(8,128)(2,1)} copy(bf16[4,32,512]{2,0,1:T(4,128)(2,1)S(1)} %convolution_convert_fusion.3) | data formatting | bytes 262144 | tf_op jit(solution)/shard_map/convert_element_type | solution.py:33
  41.9 0.0 all-to-all-done
  41.9 4.6 %all-to-all-start.1 = ((bf16[4,32,512]{2,1,0:T(8,128)(2,1)}), bf16[4,32,512]{2,1,0:T(8,128)(2,1)S(1)}, u32[]{:S(2)}, u32[]{:S(2)}) async-start(bf16[4,32,512]{2,1,0:T(8,128)(2,1)} %copy.24), calls=%async_computation.1 | async-start | bytes 262144 | tf_op jit(solution)/shard_map/all_to_all | solution.py:38
  46.6 0.1 convert_reduce_fusion
  46.7 6.2 %all-to-all-done.1 = bf16[4,32,512]{2,1,0:T(8,128)(2,1)S(1)} async-done(((bf16[4,32,512]{2,1,0:T(8,128)(2,1)}), bf16[4,32,512]{2,1,0:T(8,128)(2,1)S(1)}, u32[]{:S(2)}, u32[]{:S(2)}) %all-to-all-start.1) | async-done | bytes 131104 | tf_op jit(solution)/shard_map/all_to_all | solution.py:38
  52.8 0.5 convolution_convert_fusion.1
  53.3 0.1 reshape.90
  53.4 0.2 copy.26
  53.6 0.1 copy.27
  53.7 3.7 %convolution_convert_fusion.2 = bf16[128,1024]{1,0:T(8,128)(2,1)} fusion(bf16[128,2048]{1,0:T(8,128)(2,1)S(1)} %bitcast.34, bf16[2048,1024]{1,0:T(8,128)(2,1)} %param.9), kind=kOutput, calls=%fused_computation.3 | convolution fusion | flops 537001984 | bytes 4980736 | tf_op jit(solution)/shard_map/dot_general | solution.py:54
  (4 shorter events, 0.0 us)
Async XLA Ops:
  6.5 28.8 %all-gather.3.cloned.1.call-start = ((), (), s32[]{:S(2)}) async-start(), calls=%async_computation.2 | async-start | bytes 1179648 | tf_op jit(solution)/shard_map/all_gather | solution.py:18
  9.4 32.5 %all-to-all-start = ((bf16[4,1,1]{2,1,0:T(2,128)(2,1)}), bf16[4,1,1]{2,1,0:T(2,128)(2,1)S(1)}, u32[]{:S(2)}, u32[]{:S(2)}) async-start(bf16[4,1,1]{2,1,0:T(2,128)(2,1)} %copy.20), calls=%async_computation | async-start | bytes 4096 | tf_op jit(solution)/shard_map/all_to_all | solution.py:39
  37.1 3.7 %copy-start = (s32[1,1,16]{2,1,0:T(1,128)S(1)}, s32[1,1,16]{2,1,0:T(1,128)}, u32[]{:S(2)}) copy-start(s32[1,1,16]{2,1,0:T(1,128)} %param.10) | copy-start | bytes 196
  41.9 10.9 %all-to-all-start.1 = ((bf16[4,32,512]{2,1,0:T(8,128)(2,1)}), bf16[4,32,512]{2,1,0:T(8,128)(2,1)S(1)}, u32[]{:S(2)}, u32[]{:S(2)}) async-start(bf16[4,32,512]{2,1,0:T(8,128)(2,1)} %copy.24), calls=%async_computation.1 | async-start | bytes 262144 | tf_op jit(solution)/shard_map/all_to_all | solution.py:38
Sparse Core Ops, SparseCore 0:
  9.2 26.0 all-gather.2
where the time goes:
time: 64.6 us; the launch traced here: 64.2 us
  waiting for transfers between devices  25.2 us (39%)
  between operations  13.5 us (21%)
  starting transfers between devices  11 us (17%)
  matrix products  7.44 us (12%)
  local copies, waits for them, and re-layouts  4.21 us (7%)
  other arithmetic  2.98 us (5%)
    all_gather x1, waiting for transfers between devices, on_device(): every = lax.all_gather(amplitudes[None], 'virt', axis=0, tiled=True)  18.3 us
    all_to_all x1, starting transfers between devices, on_device(): lax.all_to_all(output_marker, 'occ', split_axis=0, concat_axis=0, tiled=T...  6.35 us
    all_to_all x1, waiting for transfers between devices, on_device(): lax.all_to_all(outgoing, 'occ', split_axis=0, concat_axis=0, tiled=True)  6.18 us
    all_to_all x1, starting transfers between devices, on_device(): lax.all_to_all(outgoing, 'occ', split_axis=0, concat_axis=0, tiled=True)  4.6 us
    dot_general x1, matrix products, on_device(): jnp.dot(left, inter, preferred_element_type=jnp.float32)  3.65 us
    dot_general x1, matrix products, on_device(): jnp.dot(chosen_entries, integrals, preferred_element_type=jnp.float32)  2.93 us
    gather x1, local copies, waits for them, and re-layouts, on_device(): chosen_entries = jnp.take(every, panel_owner[0], axis=0)  1.79 us
  transfers between devices with their start and end apart: 3, of which 2 were waited for; matrix products, arithmetic and copies ran while one was open for 16% of the time, Pallas kernels for 0%

commit v1 on v0

--- a/solution.py
+++ b/solution.py
@@ -15,7 +15,9 @@
     n_occ = lax.axis_size("occ")
     half_splits = op_rows // SROWS
     col_tiles = cols // tile
-    every = lax.all_gather(amplitudes[None], "virt", axis=0, tiled=True)
+    block = amplitudes[None]
+    stack = jnp.stack([block] * lax.axis_size("virt"))
+    every = jnp.concatenate(lax.all_to_all(stack, "virt", 0, 0), axis=0)
     chosen_entries = jnp.take(every, panel_owner[0], axis=0)
     chosen_entries = chosen_entries.transpose(1, 0, 2).reshape(op_rows, steps * tile)
     accum = jnp.dot(chosen_entries, integrals, preferred_element_type=jnp.float32)

time: 64.6 us -> 48.8 us (0.76)
  between operations: 13.5 us -> 0.09 us
  waiting for transfers between devices: 25.2 us -> 17.9 us
  starting transfers between devices: 11 us -> 15 us
  local copies, waits for them, and re-layouts: 4.21 us -> 4.94 us
    all_gather x1 -> x0, waiting for transfers between devices: 18.3 us -> none  [on_device(): every = lax.all_gather(amplitudes[None], 'virt', axis=0, tiled=True)]
    all_to_all x0 -> x1, waiting for transfers between devices: none -> 11.9 us  [on_device(): every = jnp.concatenate(lax.all_to_all(stack, 'virt', 0, 0), axis=0)]
    all_to_all x0 -> x1, starting transfers between devices: none -> 5.2 us  [on_device(): every = jnp.concatenate(lax.all_to_all(stack, 'virt', 0, 0), axis=0)]
    another operation x0 -> x1, local copies, waits for them, and re-layouts: none -> 1.97 us  [on_device(): stack = jnp.stack([block] * lax.axis_size('virt'))]
    all_to_all x1, starting transfers between devices: 6.35 us -> 4.87 us  [on_device(): lax.all_to_all(output_marker, 'occ', split_axis=0, concat_axis=0, tiled=T...]
    gather x1, local copies, waits for them, and re-layouts: 1.79 us -> 0.56 us  [on_device(): chosen_entries = jnp.take(every, panel_owner[0], axis=0)]
    unnamed x1 -> x0, waiting for transfers between devices: 0.71 us -> none
  transfers between devices with their start and end apart: 3 -> 3, of which waited for: 2 -> 3; matrix products, arithmetic and copies ran while one was open for 16% -> 18% of each run, Pallas kernels for 0% -> 0%
where the time goes in v1:
time: 48.8 us; the launch traced here: 48.4 us
  waiting for transfers between devices  17.9 us (37%)
  starting transfers between devices  15 us (31%)
  matrix products  7.44 us (15%)
  local copies, waits for them, and re-layouts  4.94 us (10%)
  other arithmetic  2.98 us (6%)
    all_to_all x1, waiting for transfers between devices, on_device(): every = jnp.concatenate(lax.all_to_all(stack, 'virt', 0, 0), axis=0)  11.9 us
    all_to_all x1, waiting for transfers between devices, on_device(): lax.all_to_all(outgoing, 'occ', split_axis=0, concat_axis=0, tiled=True)  5.8 us
    all_to_all x1, starting transfers between devices, on_device(): every = jnp.concatenate(lax.all_to_all(stack, 'virt', 0, 0), axis=0)  5.2 us
    all_to_all x1, starting transfers between devices, on_device(): lax.all_to_all(outgoing, 'occ', split_axis=0, concat_axis=0, tiled=True)  4.89 us
    all_to_all x1, starting transfers between devices, on_device(): lax.all_to_all(output_marker, 'occ', split_axis=0, concat_axis=0, tiled=T...  4.87 us
    dot_general x1, matrix products, on_device(): jnp.dot(left, inter, preferred_element_type=jnp.float32)  3.65 us
    dot_general x1, matrix products, on_device(): jnp.dot(chosen_entries, integrals, preferred_element_type=jnp.float32)  2.93 us
    another operation x1, local copies, waits for them, and re-layouts, on_device(): stack = jnp.stack([block] * lax.axis_size('virt'))  1.97 us
  transfers between devices with their start and end apart: 3, of which 3 were waited for; matrix products, arithmetic and copies ran while one was open for 18% of the time, Pallas kernels for 0%

profile of v1, /device:TPU:0, one launch (start us, length us, event | category | flops | bytes accessed | tf_op | source)
XLA Modules:
  0.0 48.4 jit_solution(9759538396323521073)
XLA Ops:
  0.0 2.0 %stack.3 = bf16[8,1,128,512]{3,2,1,0:T(8,128)(2,1)} broadcast(bf16[128,512]{1,0:T(8,128)(2,1)} %param.6), dimensions={2,3} | broadcast | bytes 1179648 | tf_op jit(solution)/shard_map/stack | solution.py:19
  2.0 5.2 %all-to-all-start.1 = ((bf16[8,1,128,512]{3,2,1,0:T(8,128)(2,1)}), bf16[8,1,128,512]{3,2,1,0:T(8,128)(2,1)S(1)}, u32[]{:S(2)}, u32[]{:S(2)}) async-start(bf16[8,1,128,512]{3,2,1,0:T(8,128)(2,1)} %stack.3), calls=%async_computation.1 | async-start | bytes 2097152 | tf_op jit(solution)/shard_map/all_to_all | solution.py:20
  7.2 0.7 %compare_bitcast_fusion = pred[16]{0:T(512)(128)(4,1)S(1)} fusion(s32[1,1,16]{2,1,0:T(1,128)} %param.11), kind=kLoop, calls=%fused_computation.19 | loop fusion | flops 16 | bytes 80 | tf_op jit(solution)/shard_map/eq | solution.py:32
  7.8 0.8 %select_reduce_fusion = s32[4]{0:T(128)S(1)} fusion(s32[16]{0:T(128)S(1)} %iota_add_fusion, s32[16]{0:T(128)} %bitcast.39, pred[16]{0:T(512)(128)(4,1)S(1)} %compare_bitcast_fusion), kind=kLoop, calls=%fused_computation.12 | loop fusion | flops 252 | bytes 160 | tf_op jit(solution)/shard_map/reduce_sum | solution.py:36
  8.6 0.7 %copy.20 = bf16[4,1,1]{2,1,0:T(2,128)(2,1)} copy(bf16[4,1,1]{0,2,1:T(2,128)(2,1)S(1)} %convert_bitcast_fusion) | data formatting | bytes 16 | tf_op jit(solution)/shard_map/convert_element_type | solution.py:36
  9.3 0.7 %fusion.11 = s32[2]{0:T(128)S(1)} fusion(s32[1,2]{1,0:T(1,128)} %param.8), kind=kLoop, calls=%fused_computation.24 | loop fusion | flops 6 | bytes 16 | tf_op jit(solution)/shard_map/jit(_take)/jit(_where)/select_n | solution.py:21
  10.0 0.7 %compare_and_fusion = pred[2]{0:T(512)(128)(4,1)S(1)} fusion(s32[1,2]{1,0:T(1,128)} %param.8), kind=kLoop, calls=%fused_computation.17 | loop fusion | flops 12 | bytes 10 | tf_op jit(solution)/shard_map/jit(_take)/and | solution.py:21
  10.6 11.9 %all-to-all-done.1 = bf16[8,1,128,512]{3,2,1,0:T(8,128)(2,1)S(1)} async-done(((bf16[8,1,128,512]{3,2,1,0:T(8,128)(2,1)}), bf16[8,1,128,512]{3,2,1,0:T(8,128)(2,1)S(1)}, u32[]{:S(2)}, u32[]{:S(2)}) %all-to-all-start.1) | async-done | bytes 1048608 | tf_op jit(solution)/shard_map/all_to_all | solution.py:20
  22.5 4.9 %all-to-all-start = ((bf16[4,1,1]{2,1,0:T(2,128)(2,1)}), bf16[4,1,1]{2,1,0:T(2,128)(2,1)S(1)}, u32[]{:S(2)}, u32[]{:S(2)}) async-start(bf16[4,1,1]{2,1,0:T(2,128)(2,1)} %copy.20), calls=%async_computation | async-start | bytes 4096 | tf_op jit(solution)/shard_map/all_to_all | solution.py:41
  27.4 0.6 %gather_fusion = bf16[2,128,512]{2,1,0:T(8,128)(2,1)S(1)} fusion(bf16[8,128,512]{2,1,0:T(8,128)(2,1)S(1)} %bitcast.37, s32[1024]{0:T(1024)S(1)} %pad_clamp_fusion), kind=kCustom, calls=%fused_computation | custom fusion | bytes 524296 | tf_op jit(solution)/shard_map/jit(_take)/gather | solution.py:21
  28.0 0.0 copy-start
  28.0 0.1 select_bitcast_fusion
  28.1 0.2 copy.21
  28.3 2.9 %convolution_convert_fusion = bf16[128,2048]{1,0:T(8,128)(2,1)S(1)} fusion(bf16[128,1024]{0,1:T(8,128)(2,1)S(1)} %bitcast.38, bf16[1024,2048]{1,0:T(8,128)(2,1)} %param.7), kind=kOutput, calls=%fused_computation.1 | convolution fusion | flops 537133056 | bytes 4980736 | tf_op jit(solution)/shard_map/dot_general | solution.py:23
  31.2 0.4 reshape.94
  31.6 0.1 copy.22
  31.7 0.0 copy-done
  31.7 0.4 convolution_convert_fusion.3
  32.1 0.7 %copy.24 = bf16[4,32,512]{2,1,0:T(8,128)(2,1)} copy(bf16[4,32,512]{2,0,1:T(4,128)(2,1)S(1)} %convolution_convert_fusion.3) | data formatting | bytes 262144 | tf_op jit(solution)/shard_map/convert_element_type | solution.py:35
  32.8 0.2 all-to-all-done
  33.0 4.9 %all-to-all-start.2 = ((bf16[4,32,512]{2,1,0:T(8,128)(2,1)}), bf16[4,32,512]{2,1,0:T(8,128)(2,1)S(1)}, u32[]{:S(2)}, u32[]{:S(2)}) async-start(bf16[4,32,512]{2,1,0:T(8,128)(2,1)} %copy.24), calls=%async_computation.2 | async-start | bytes 262144 | tf_op jit(solution)/shard_map/all_to_all | solution.py:40
  37.9 0.1 convert_reduce_fusion
  38.0 5.8 %all-to-all-done.2 = bf16[4,32,512]{2,1,0:T(8,128)(2,1)S(1)} async-done(((bf16[4,32,512]{2,1,0:T(8,128)(2,1)}), bf16[4,32,512]{2,1,0:T(8,128)(2,1)S(1)}, u32[]{:S(2)}, u32[]{:S(2)}) %all-to-all-start.2) | async-done | bytes 131104 | tf_op jit(solution)/shard_map/all_to_all | solution.py:40
  43.8 0.5 convolution_convert_fusion.1
  44.3 0.1 reshape.96
  44.4 0.2 copy.26
  44.6 0.1 copy.27
  44.7 3.7 %convolution_convert_fusion.2 = bf16[128,1024]{1,0:T(8,128)(2,1)} fusion(bf16[128,2048]{1,0:T(8,128)(2,1)S(1)} %bitcast.34, bf16[2048,1024]{1,0:T(8,128)(2,1)} %param.9), kind=kOutput, calls=%fused_computation.3 | convolution fusion | flops 537001984 | bytes 4980736 | tf_op jit(solution)/shard_map/dot_general | solution.py:56
  (4 shorter events, 0.0 us)
Async XLA Ops:
  2.0 20.6 %all-to-all-start.1 = ((bf16[8,1,128,512]{3,2,1,0:T(8,128)(2,1)}), bf16[8,1,128,512]{3,2,1,0:T(8,128)(2,1)S(1)}, u32[]{:S(2)}, u32[]{:S(2)}) async-start(bf16[8,1,128,512]{3,2,1,0:T(8,128)(2,1)} %stack.3), calls=%async_computation.1 | async-start | bytes 2097152 | tf_op jit(solution)/shard_map/all_to_all | solution.py:20
  22.5 10.4 %all-to-all-start = ((bf16[4,1,1]{2,1,0:T(2,128)(2,1)}), bf16[4,1,1]{2,1,0:T(2,128)(2,1)S(1)}, u32[]{:S(2)}, u32[]{:S(2)}) async-start(bf16[4,1,1]{2,1,0:T(2,128)(2,1)} %copy.20), calls=%async_computation | async-start | bytes 4096 | tf_op jit(solution)/shard_map/all_to_all | solution.py:41
  28.0 3.7 %copy-start = (s32[1,1,16]{2,1,0:T(1,128)S(1)}, s32[1,1,16]{2,1,0:T(1,128)}, u32[]{:S(2)}) copy-start(s32[1,1,16]{2,1,0:T(1,128)} %param.10) | copy-start | bytes 196
  33.0 10.8 %all-to-all-start.2 = ((bf16[4,32,512]{2,1,0:T(8,128)(2,1)}), bf16[4,32,512]{2,1,0:T(8,128)(2,1)S(1)}, u32[]{:S(2)}, u32[]{:S(2)}) async-start(bf16[4,32,512]{2,1,0:T(8,128)(2,1)} %copy.24), calls=%async_computation.2 | async-start | bytes 262144 | tf_op jit(solution)/shard_map/all_to_all | solution.py:40
